TPU v7x, 128 devices: a whole 4x4x4 slice. The times are simulated.
128 devices in a mesh: req: 8 (over x, core), mlp: 16 (over z, y).
Axes of the slice: x: 4, y: 4, z: 4, core: 2. Of those that a mesh axis runs over, the one named last changes fastest.
Arguments:
- tokens: bfloat16 [8192, 4096], P(('req', 'mlp')), may hold values from -6 to 6
- layer_norm_gain: float32 [4096], replicated, may hold values from 0.1 to 1.9
- layer_norm_bias: float32 [4096], replicated, may hold values from -2 to 2
- query_key_weight: bfloat16 [4096, 16, 768], P(None, 'mlp')
- output_weight: bfloat16 [16, 256, 4096], P('mlp'), may hold values from -0.09375 to 0.09375
- up_weight: bfloat16 [4096, 8192], P(None, 'mlp'), may hold values from -0.09375 to 0.09375
- input_bias: float32 [8192], P('mlp'), may hold values from -3 to 3
- down_weight: bfloat16 [8192, 4096], P('mlp'), may hold values from -0.0625 to 0.0625
- output_bias: float32 [4096], replicated, may hold values from -2 to 2
- input_adapter_left: bfloat16 [4096, 2048], P(None, 'mlp'), may hold values from -0.09375 to 0.09375
- query_key_value_right: bfloat16 [1024, 16, 768], P(None, 'mlp'), may hold values from -1.5 to 1.5
- up_adapter_right: bfloat16 [1024, 8192], P(None, 'mlp'), may hold values from -1.5 to 1.5
- output_adapter_left: bfloat16 [16, 256, 1024], P('mlp'), may hold values from -0.09375 to 0.09375
- down_adapter_left: bfloat16 [8192, 1024], P('mlp'), may hold values from -0.0625 to 0.0625
- output_adapter_right: bfloat16 [2048, 4096], P('mlp'), may hold values from -1 to 1
- lengths: int32 [257], replicated, may hold values from 8 to 4096, as said below
- request_adapter: int32 [257], replicated, may hold values from 0 to 63
- slot_adapter: int32 [64], P('mlp'), may hold values from 0 to 63, each once
Outputs:
- mixed: bfloat16 [8192, 4096], P(('req', 'mlp'))
Inputs may be any that keep to these rules, and one draw needn't show every extreme that they name: `lengths`: one request holds exactly 4096 tokens, every other one 8 to 24; together they hold 8192 tokens. `slot_adapter`: every adapter id stands in exactly one slot.
All inputs are finite; a program needn't handle non-finite values.
Results may differ from a plain program's by a relative error of at most 0.017.
Values may be sent and summed in bfloat16 or wider, within the bound.
A program may use at most 128 MiB of HBM per device.

v0:
```python
import math
import jax
import jax.numpy as jnp
from jax import lax
from jax.sharding import PartitionSpec as P

HEAD_SIZE = 256
ROT = 64
ADAPTER_RANK = 16
ADP_DEV = 4
EPSILON = 1e-05
NEGATIVE_FILL = -1e30


def rank_product(left_side, right_side):
    return jnp.dot(left_side, right_side, preferred_element_type=jnp.float32)


def normalize(inputs, layer_norm_gain, layer_norm_bias):
    values = inputs.astype(jnp.float32)
    center = values - jnp.mean(values, axis=1, keepdims=True)
    spread = jnp.mean(center * center, axis=1, keepdims=True)
    scaled = center * lax.rsqrt(spread + EPSILON)
    return (scaled * layer_norm_gain + layer_norm_bias).astype(jnp.bfloat16)


def token_info(lengths, request_adapter, first_row, row_count):
    endings = jnp.cumsum(lengths)
    anchors = endings - lengths
    token_index = first_row + lax.iota(jnp.int32, row_count)
    inside = anchors[None, :] <= token_index[:, None]
    request = jnp.sum(inside.astype(jnp.int32), axis=1) - 1
    request_start = jnp.max(jnp.where(inside, anchors[None, :], jnp.zeros((), jnp.int32)), axis=1)
    adapter_id = jnp.take(request_adapter, jnp.maximum(request, 0))
    return (token_index, request, token_index - request_start, adapter_id)


def rotate(matrix, position):
    row_count = matrix.shape[0]
    head_count = matrix.shape[1]
    half_rot = ROT // 2
    frequency = jnp.exp(jnp.arange(half_rot, dtype=jnp.float32) * (-2.0 * math.log(10000.0) / ROT))
    angles = position.astype(jnp.float32)[:, None] * frequency[None, :]
    cosine = jnp.cos(angles)[:, None, :]
    sine_value = jnp.sin(angles)[:, None, :]
    paired_part = matrix[:, :, :ROT].reshape(row_count, head_count, half_rot, 2)
    even_part = paired_part[:, :, :, 0]
    odd_part = paired_part[:, :, :, 1]
    turned = jnp.stack(
        [even_part * cosine - odd_part * sine_value, odd_part * cosine + even_part * sine_value],
        axis=-1,
    )
    return jnp.concatenate([turned.reshape(row_count, head_count, ROT), matrix[:, :, ROT:]], axis=2)


def slot_selector(products, chosen, adapter_id, column_count):
    row_count = products.shape[0]
    selector = (adapter_id[:, None] == chosen[None, :]).astype(jnp.float32)
    reshaped = products.reshape(row_count, chosen.shape[0], column_count)
    return jnp.sum(selector[:, :, None] * reshaped, axis=1)


def widen_rows(values, chosen, adapter_id):
    selector = adapter_id[:, None] == chosen[None, :]
    spread = jnp.where(selector[:, :, None], values[:, None, :], jnp.zeros((), values.dtype))
    return spread.reshape(values.shape[0], chosen.shape[0] * values.shape[1])


def per_device(
    tokens,
    layer_norm_gain,
    layer_norm_bias,
    query_key_weight,
    output_weight,
    up_weight,
    input_bias,
    down_weight,
    output_bias,
    input_adapter_left,
    query_key_value_right,
    up_adapter_right,
    output_adapter_left,
    down_adapter_left,
    output_adapter_right,
    lengths,
    request_adapter,
    slot_adapter,
):
    tok_dev = tokens.shape[0]
    model_width = tokens.shape[1]
    mlp_count = lax.axis_size("mlp")
    tok_grp = tok_dev * mlp_count
    group_first = lax.axis_index("req") * tok_grp
    heads_local = query_key_weight.shape[1]
    hid_local = up_weight.shape[1]
    adapter_ids = slot_adapter.shape[0] * mlp_count
    every_id = lax.iota(jnp.int32, adapter_ids)
    query_key_columns = heads_local * 3 * HEAD_SIZE
    attention_columns = heads_local * HEAD_SIZE
    query_key_rows = query_key_weight.reshape(model_width, query_key_columns)
    normed_rows = normalize(tokens, layer_norm_gain, layer_norm_bias)
    slot_portion = lax.all_gather(normed_rows, "mlp", axis=0, tiled=True)
    grouped = jnp.concatenate(
        [
            rank_product(slot_portion, query_key_rows),
            rank_product(slot_portion, up_weight),
            rank_product(slot_portion, input_adapter_left),
        ],
        axis=1,
    )
    token_index, request, position, adapter_id = token_info(
        lengths, request_adapter, group_first, tok_grp
    )
    rank_part = slot_selector(
        grouped[:, query_key_columns + hid_local :], slot_adapter, adapter_id, 2 * ADAPTER_RANK
    )
    rank_input = lax.psum(rank_part.astype(jnp.bfloat16), "mlp")
    qkv_extra = rank_product(
        widen_rows(rank_input[:, :ADAPTER_RANK], every_id, adapter_id),
        query_key_value_right.reshape(adapter_ids * ADAPTER_RANK, query_key_columns),
    )
    up_delta = rank_product(
        widen_rows(rank_input[:, ADAPTER_RANK:], every_id, adapter_id), up_adapter_right
    )
    projected_rows = (grouped[:, :query_key_columns] + qkv_extra).reshape(
        tok_grp, heads_local, 3 * HEAD_SIZE
    )
    hidden_units = jax.nn.gelu(
        grouped[:, query_key_columns : query_key_columns + hid_local] + up_delta + input_bias,
        approximate=True,
    ).astype(jnp.bfloat16)
    queries = rotate(projected_rows[:, :, :HEAD_SIZE], position).astype(jnp.bfloat16)
    key_rows = (
        rotate(projected_rows[:, :, HEAD_SIZE : 2 * HEAD_SIZE], position)
        .astype(jnp.bfloat16)
        .reshape(tok_grp, attention_columns)
    )
    value_rows = (
        projected_rows[:, :, 2 * HEAD_SIZE :]
        .astype(jnp.bfloat16)
        .reshape(tok_grp, attention_columns)
    )
    paired = jnp.stack([key_rows, value_rows])
    score_scale = HEAD_SIZE ** (-0.5)
    last_row = group_first + tok_grp - 1
    start_state = (
        jnp.full((tok_grp, heads_local), NEGATIVE_FILL, jnp.float32),
        jnp.zeros((tok_grp, heads_local), jnp.float32),
        jnp.zeros((tok_grp, heads_local, HEAD_SIZE), jnp.float32),
    )
    slot_portion = lax.all_gather(paired, "req", axis=1, tiled=True)
    offset = jnp.int32(0)
    amount = slot_portion.shape[1]
    key_index, key_request, key_position, key_adapter = token_info(
        lengths, request_adapter, offset, amount
    )
    useful = jnp.logical_and(offset <= last_row, key_request[amount - 1] >= request[0])

    def attend(current):
        running_top, running_total, running_sum = current
        part_keys = slot_portion[0].reshape(amount, heads_local, HEAD_SIZE)
        part_values = slot_portion[1].reshape(amount, heads_local, HEAD_SIZE)
        scores = (
            jnp.einsum("qhd,khd->qhk", queries, part_keys, preferred_element_type=jnp.float32)
            * score_scale
        )
        allowed = jnp.logical_and(
            key_request[None, :] == request[:, None], key_index[None, :] <= token_index[:, None]
        )[:, None, :]
        masked = jnp.where(allowed, scores, NEGATIVE_FILL)
        new_top = jnp.maximum(running_top, jnp.max(masked, axis=2))
        weights = jnp.where(allowed, jnp.exp(masked - new_top[:, :, None]), 0.0)
        new_total = jnp.sum(weights, axis=2)
        new_sum = jnp.einsum(
            "qhk,khd->qhd",
            weights.astype(jnp.bfloat16),
            part_values,
            preferred_element_type=jnp.float32,
        )
        return (new_top, new_total, new_sum)

    final_state = lax.cond(useful, attend, lambda current: current, start_state)
    attention_output = (
        (final_state[2] / final_state[1][:, :, None])
        .astype(jnp.bfloat16)
        .reshape(tok_grp, attention_columns)
    )
    output_rows = output_weight.reshape(attention_columns, model_width)
    own_ids = lax.axis_index("mlp") * ADP_DEV + lax.iota(jnp.int32, ADP_DEV)
    output_rank_rows = rank_product(
        attention_output, output_adapter_left.reshape(attention_columns, adapter_ids * ADAPTER_RANK)
    )
    down_rank_rows = rank_product(hidden_units, down_adapter_left)
    rank_part_out = jnp.concatenate(
        [
            slot_selector(output_rank_rows, every_id, adapter_id, ADAPTER_RANK),
            slot_selector(down_rank_rows, every_id, adapter_id, ADAPTER_RANK),
        ],
        axis=1,
    )
    rank_output = lax.psum(rank_part_out.astype(jnp.bfloat16), "mlp")
    rank_widened = widen_rows(rank_output, own_ids, adapter_id)
    mixed = lax.psum_scatter(
        (
            rank_product(attention_output, output_rows)
            + (
                rank_product(hidden_units, down_weight)
                + rank_product(rank_widened, output_adapter_right)
            )
        ).astype(jnp.bfloat16),
        "mlp",
        scatter_dimension=0,
        tiled=True,
    ).astype(jnp.float32)
    return (mixed + tokens.astype(jnp.float32) + output_bias).astype(jnp.bfloat16)


def solution(mesh):
    in_specs = (
        P(("req", "mlp"), None),
        P(),
        P(),
        P(None, "mlp", None),
        P("mlp", None, None),
        P(None, "mlp"),
        P("mlp"),
        P("mlp", None),
        P(),
        P(None, "mlp"),
        P(None, "mlp", None),
        P(None, "mlp"),
        P("mlp", None, None),
        P("mlp", None),
        P("mlp", None),
        P(),
        P(),
        P("mlp"),
    )
    out_specs = P(("req", "mlp"), None)
    return jax.shard_map(
        per_device, mesh=mesh, in_specs=in_specs, out_specs=out_specs, check_vma=False
    )
```

profile of v0, /device:TPU:0, one launch (start us, length us, event | category | flops | bytes accessed | tf_op | source)
XLA Modules:
  0.0 493.8 jit_solution(12925493245137740278)
XLA Ops:
  6.5 1.4 convert_reduce_fusion.1
  7.9 1.3 fusion.35
  9.3 2.1 fusion.38
  11.5 0.7 pad_bitcast_fusion
  12.8 0.7 slice_subtract_fusion
  13.8 6.2 %gather_fusion = s32[1024]{0:T(1024)S(1)} fusion(s32[257]{0:T(512)} %param.36, s32[1024]{0:T(1024)S(1)} %maximum_clamp_fusion), kind=kCustom, calls=%fused_computation | custom fusion | bytes 12288 | tf_op jit(solution)/shard_map/jit(_take)/gather | solution.py:34
  20.1 0.8 fusion.60
  20.8 64.1 %all-gather.3.cloned.1.call-done = bf16[1024,4096]{1,0:T(8,128)(2,1)} async-done(((bf16[64,4096]{1,0:T(8,128)(2,1)}), bf16[1024,4096]{1,0:T(8,128)(2,1)}) %all-gather.3.cloned.1.call-update) | async-done | bytes 8388624 | tf_op jit(solution)/shard_map/all_gather | solution.py:102
  84.9 6.3 %fusion.67 = f32[1024,128]{0,1:T(8,128)S(1)} fusion(bf16[1024,4096]{1,0:T(8,128)(2,1)} %all-gather.3.cloned.1.call-done, bf16[4096,128]{1,0:T(8,128)(2,1)S(1)} %copy-done.2), kind=kOutput, calls=%fused_computation.113 | convolution fusion | flops 1073741824 | bytes 9961472 | tf_op jit(solution)/shard_map/dot_general | solution.py:16
  91.2 0.7 multiply_reduce_fusion.1
  92.5 80.1 %all-reduce.4.cloned.1.call-done = bf16[1024,32]{0,1:T(8,128)(2,1)} async-done(((bf16[1024,32]{0,1:T(8,128)(2,1)}), bf16[1024,32]{0,1:T(8,128)(2,1)}) %all-reduce.4.cloned.1.call-update) | async-done | bytes 65552 | tf_op jit(solution)/shard_map/psum | solution.py:117
  172.6 0.8 fusion.65
  173.4 1.8 broadcast_select_fusion
  175.2 3.3 fusion.29
  178.5 11.0 %fusion.66 = (bf16[1024,1,768]{0,2,1:T(8,128)(2,1)S(1)}, f32[1024,1,768]{0,2,1:T(8,128)S(1)}) fusion(f32[1024,768]{0,1:T(8,128)S(1)} %fusion.29, bf16[1024,4096]{1,0:T(8,128)(2,1)} %all-gather.3.cloned.1.call-done, bf16[4096,1,768]{2,0,1:T(8,128)(2,1)} %param.23), kind=kOutput, calls=%fused_computation.112 | convolution fusion | flops 6444023808 | bytes 22544384 | tf_op jit(solution)/shard_map/dot_general | solution.py:16
  189.6 0.8 fusion.61
  190.4 2.0 reshape.569
  192.4 1.6 fusion.63
  194.0 2.0 reshape.568
  196.0 1.0 fusion.64
  197.0 2.2 fusion.57
  199.2 0.8 copy.41
  200.0 1.0 concatenate.35
  200.9 1.1 pad_maximum_fusion
  202.3 0.6 slice.68
  202.9 1.3 convert_reduce_fusion
  204.2 0.6 slice.84
  206.1 2.0 copy.47
  208.2 11.3 %fusion.68 = f32[1024,512]{1,0:T(8,128)} fusion(bf16[1024,4096]{1,0:T(8,128)(2,1)} %all-gather.3.cloned.1.call-done, bf16[4096,512]{1,0:T(8,128)(2,1)} %param.25), kind=kOutput, calls=%fused_computation.114 | convolution fusion | flops 4294967296 | bytes 14680064 | tf_op jit(solution)/shard_map/dot_general | solution.py:16
  219.7 0.8 pad_maximum_fusion.1
  220.6 4.5 fusion.24
  225.1 1.3 fusion.70
  226.5 2.4 fusion.16
  228.9 8.3 %fusion.69 = f32[1024,4096]{1,0:T(8,128)} fusion(bf16[1024,512]{1,0:T(8,128)(2,1)S(1)} %fusion.24, bf16[512,4096]{1,0:T(8,128)(2,1)S(1)} %copy-done.9), kind=kOutput, calls=%fused_computation.115 | convolution fusion | flops 4294967296 | bytes 22020096 | tf_op jit(solution)/shard_map/dot_general | solution.py:16
  237.2 14.0 %all-gather.5.cloned.1.call-done = bf16[2,8192,256]{1,2,0:T(8,128)(2,1)} async-done(((bf16[2,1024,256]{1,2,0:T(8,128)(2,1)}), bf16[2,8192,256]{1,2,0:T(8,128)(2,1)}) %all-gather.5.cloned.1.call-update) | async-done | bytes 8388624 | tf_op jit(solution)/shard_map/all_gather | solution.py:151
  251.2 49.0 %conditional.1 = (f32[1024,1]{0,1:T(1,128)S(1)}, f32[1024,1,256]{2,0,1:T(8,128)S(1)}) conditional(s32[]{:T(128)} %convert_element_type.83, () %tuple.13, (s32[8192]{0:T(1024)S(1)}, s32[1024]{0:T(1024)S(1)}, s32[8192]{0:T(1024)S(1)}, s32[]{:T(128)}, s32[1024]{0:T(1024)S(1)}, /*index=5*/bf16[2,8192,256]{1,2,0:T(8,128)(2,1)}, ...), branch_computations={%region_9.10_spmd, %region_10.13_spmd} | conditional | flops 8774483968 | bytes 129753136 | solution.py:182
  251.2 12.0 %copy.45 = bf16[2,8192,256]{2,1,0:T(8,128)(2,1)} copy(bf16[2,8192,256]{1,2,0:T(8,128)(2,1)} %get-tuple-element.65) | data formatting | bytes 16777216 | tf_op jit(solution)/shard_map
  263.2 10.0 %fusion = (f32[1024]{0:T(1024)S(1)}, f32[8192,1024]{1,0:T(8,128)S(1)}) fusion(s32[1024]{0:T(1024)S(1)} %broadcast_add_fusion, s32[1024]{0:T(1024)S(1)} %get-tuple-element.22, s32[8192]{0:T(1024)S(1)} %get-tuple-element.23, s32[8192]{0:T(1024)S(1)} %get-tuple-element.21, bf16[1024,1,256]{0,2,1:T(8,128)(2,1)S(1)} %copy-done.4, bf16[2,8192,256]{2,1,0:T(8,128)(2,1)} %copy.45), kind=kOutput, calls=%fused_computation.4 | convolution fusion | flops 4345297920 | bytes 38350848 | tf_op jit(solution)/shard_map/cond/branch_1_fun/qhd,khd->qhk/dot_general | solution.py:164
  273.2 14.2 %fusion.7 = f32[1024,1,256]{2,0,1:T(8,128)S(1)} fusion(bf16[2,8192,256]{2,1,0:T(8,128)(2,1)} %copy.45, f32[8192,1024]{1,0:T(8,128)S(1)} %get-tuple-element.70, f32[1024]{0:T(1024)S(1)} %broadcast_maximum_fusion, s32[1024]{0:T(1024)S(1)} %broadcast_add_fusion, s32[1024]{0:T(1024)S(1)} %get-tuple-element.22, s32[8192]{0:T(1024)S(1)} %get-tuple-element.23, ...), kind=kOutput, calls=%fused_computation.12 | convolution fusion | flops 4362076160 | bytes 38875136 | tf_op jit(solution)/shard_map/cond/branch_1_fun/qhk,khd->qhd/dot_general | solution.py:174
  287.4 12.8 %fusion.2 = f32[1024]{0:T(1024)S(1)} fusion(f32[8192,1024]{1,0:T(8,128)S(1)} %get-tuple-element.70, f32[1024]{0:T(1024)S(1)} %broadcast_maximum_fusion, s32[1024]{0:T(1024)S(1)} %broadcast_add_fusion, s32[1024]{0:T(1024)S(1)} %get-tuple-element.22, s32[8192]{0:T(1024)S(1)} %get-tuple-element.23, s32[8192]{0:T(1024)S(1)} %get-tuple-element.21), kind=kLoop, calls=%fused_computation.6 | loop fusion | flops 67107840 | bytes 33636352 | tf_op jit(solution)/shard_map/cond/branch_1_fun/reduce_sum | solution.py:173
  300.2 1.9 multiply_reduce_fusion
  302.2 0.6 pad_maximum_fusion.4
  302.9 8.1 %fusion.25 = f32[1024,4096]{1,0:T(8,128)} fusion(bf16[1,256,4096]{2,1,0:T(8,128)(2,1)S(1)} %copy-done, f32[1024,1,256]{2,0,1:T(8,128)S(1)} %get-tuple-element.30, f32[1024]{0:T(1024)S(1)} %bitcast.116), kind=kOutput, calls=%fused_computation.37 | convolution fusion | flops 2148007936 | bytes 19927040 | tf_op jit(solution)/shard_map/dot_general | solution.py:16
  311.0 73.2 %all-reduce.6.cloned.1.call-done = bf16[1024,32]{0,1:T(8,128)(2,1)} async-done(((bf16[1024,32]{0,1:T(8,128)(2,1)}), bf16[1024,32]{0,1:T(8,128)(2,1)}) %all-reduce.6.cloned.1.call-update) | async-done | bytes 65552 | tf_op jit(solution)/shard_map/psum | solution.py:201
  384.2 0.9 broadcast_select_fusion.2
  385.0 15.6 %add_convert_fusion = bf16[1024,4096]{1,0:T(8,128)(2,1)} fusion(f32[1024,4096]{1,0:T(8,128)} %fusion.25, f32[1024,4096]{1,0:T(8,128)} %fusion.69, bf16[1024,128]{0,1:T(8,128)(2,1)S(1)} %bitcast.112, bf16[128,4096]{1,0:T(8,128)(2,1)} %param.34), kind=kOutput, calls=%fused_computation.19 | convolution fusion | flops 1086324736 | bytes 43253760 | tf_op jit(solution)/shard_map/dot_general | solution.py:16
  400.7 84.6 %reduce-scatter.2.cloned.1.call-done = bf16[64,4096]{1,0:T(8,128)(2,1)} async-done(((bf16[1024,4096]{1,0:T(8,128)(2,1)}), bf16[64,4096]{1,0:T(8,128)(2,1)}) %reduce-scatter.2.cloned.1.call-update) | async-done | bytes 524304 | tf_op jit(solution)/shard_map/reduce_scatter | solution.py:203
  485.3 2.0 fusion.40
  (59 shorter events, 2.4 us)
Async XLA Ops:
  6.5 296.3 %copy-start = (bf16[1,256,4096]{2,1,0:T(8,128)(2,1)S(1)}, bf16[1,256,4096]{2,1,0:T(8,128)(2,1)}, u32[]{:S(2)}) copy-start(bf16[1,256,4096]{2,1,0:T(8,128)(2,1)} %param.24) | copy-start | bytes 6291460
  6.5 13.5 %copy-start.8 = (s32[4]{0:T(128)S(1)}, s32[4]{0:T(128)}, u32[]{:S(2)}) copy-start(s32[4]{0:T(128)} %param.37) | copy-start | bytes 52
  6.5 78.4 %copy-start.2 = (bf16[4096,128]{1,0:T(8,128)(2,1)S(1)}, bf16[4096,128]{1,0:T(8,128)(2,1)}, u32[]{:S(2)}) copy-start(bf16[4096,128]{1,0:T(8,128)(2,1)} %param.29) | copy-start | bytes 3145732
  6.5 78.4 %all-gather.3.cloned.1.call-start = ((), (), s32[]{:S(2)}) async-start(), calls=%async_computation.1 | async-start | bytes 8912896 | tf_op jit(solution)/shard_map/all_gather | solution.py:102
  11.4 161.2 %all-reduce.4.cloned.1.call-start = ((), (), s32[]{:S(2)}) async-start(), calls=%async_computation.2 | async-start | bytes 131072 | tf_op jit(solution)/shard_map/psum | solution.py:117
  91.9 159.3 %all-gather.5.cloned.1.call-start = ((), (), s32[]{:S(2)}) async-start(), calls=%async_computation.3 | async-start | bytes 9437184 | tf_op jit(solution)/shard_map/all_gather | solution.py:151
  202.1 182.1 %all-reduce.6.cloned.1.call-start = ((), (), s32[]{:S(2)}) async-start(), calls=%async_computation.4 | async-start | bytes 131072 | tf_op jit(solution)/shard_map/psum | solution.py:201
  208.2 11.3 %copy-start.5 = (bf16[1024,1,32,1]{0,2,3,1:T(8,128)(2,1)S(1)}, bf16[1024,1,32,1]{0,2,3,1:T(8,128)(2,1)}, u32[]{:S(2)}) copy-start(bf16[1024,1,32,1]{0,2,3,1:T(8,128)(2,1)} %get-tuple-element.75) | copy-start | bytes 196612
  208.2 11.3 %copy-start.6 = (bf16[1024,1,32,1]{0,2,3,1:T(8,128)(2,1)S(1)}, bf16[1024,1,32,1]{0,2,3,1:T(8,128)(2,1)}, u32[]{:S(2)}) copy-start(bf16[1024,1,32,1]{0,2,3,1:T(8,128)(2,1)} %get-tuple-element.76) | copy-start | bytes 196612
  208.2 12.4 %copy-start.11 = (f32[512]{0:T(512)S(1)}, f32[512]{0:T(512)}, u32[]{:S(2)}) copy-start(f32[512]{0:T(512)} %param.26) | copy-start | bytes 6148
  220.6 4.6 copy-start.10
  225.1 1.4 copy-start.3
  225.1 3.8 copy-start.9
  251.2 12.0 %copy-start.4 = (bf16[1024,1,256]{0,2,1:T(8,128)(2,1)S(1)}, bf16[1024,1,256]{0,2,1:T(8,128)(2,1)}, u32[]{:S(2)}) copy-start(bf16[1024,1,256]{0,2,1:T(8,128)(2,1)} %get-tuple-element.66) | copy-start | bytes 1572868 | tf_op jit(solution)/shard_map/cond
  302.8 182.5 %reduce-scatter.2.cloned.1.call-start = ((), (), s32[]{:S(2)}) async-start(), calls=%async_computation.5 | async-start | bytes 8912896 | tf_op jit(solution)/shard_map/reduce_scatter | solution.py:203
  400.6 84.7 %copy-start.1 = (bf16[64,4096]{1,0:T(8,128)(2,1)S(1)}, bf16[64,4096]{1,0:T(8,128)(2,1)}, u32[]{:S(2)}) copy-start(bf16[64,4096]{1,0:T(8,128)(2,1)} %param.20) | copy-start | bytes 1572868
  400.6 84.7 %copy-start.7 = (f32[4096]{0:T(1024)S(1)}, f32[4096]{0:T(1024)}, u32[]{:S(2)}) copy-start(f32[4096]{0:T(1024)} %param.28) | copy-start | bytes 49156
Sparse Core Ops, SparseCore 0:
  11.5 73.3 all-gather.2
  92.0 80.5 all-reduce.3
  202.2 48.9 all-gather.4
  302.9 81.1 all-reduce.5
  400.8 84.4 reduce-scatter.1
where the time goes:
time: 495 us; the launch traced here: 494 us
  waiting for transfers between devices  316 us (64%)
  matrix products  95.9 us (19%)
  other arithmetic  34.2 us (7%)
  local copies, waits for them, and re-layouts  32.5 us (7%)
  between operations  14.7 us (3%)
    reduce_scatter x1, waiting for transfers between devices, per_device(): lax.psum_scatter((rank_product(attention_output, output_rows) + (rank_pro...  84.6 us
    psum x1, waiting for transfers between devices, per_device(): rank_input = lax.psum(rank_part.astype(jnp.bfloat16), 'mlp')  80.1 us
    psum x1, waiting for transfers between devices, per_device(): rank_output = lax.psum(rank_part_out.astype(jnp.bfloat16), 'mlp')  73.2 us
    dot_general x10, matrix products, rank_product(): return jnp.dot(left_side, right_side, preferred_element_type=jnp.float32)  71.7 us
    all_gather x1, waiting for transfers between devices, per_device(): slot_portion = lax.all_gather(normed_rows, 'mlp', axis=0, tiled=True)  64.1 us
    dot_general x1, matrix products, attend(): jnp.einsum('qhk,khd->qhd', weights.astype(jnp.bfloat16), part_values, pre...  14.2 us
    all_gather x1, waiting for transfers between devices, per_device(): slot_portion = lax.all_gather(paired, 'req', axis=1, tiled=True)  14 us
    reduce_sum x1, other arithmetic, attend(): new_total = jnp.sum(weights, axis=2)  12.8 us
  transfers between devices with their start and end apart: 5, of which 5 were waited for; matrix products, arithmetic and copies ran while one was open for 10% of the time, Pallas kernels for 0%

commit v1 on v0

--- a/solution.py
+++ b/solution.py
@@ -148,7 +148,12 @@
         jnp.zeros((tok_grp, heads_local), jnp.float32),
         jnp.zeros((tok_grp, heads_local, HEAD_SIZE), jnp.float32),
     )
-    slot_portion = lax.all_gather(paired, "req", axis=1, tiled=True)
+    ring = [paired]
+    for hop in range(7):
+        ring.append(lax.ppermute(ring[-1], "req", [(dev, (dev + 1) % 8) for dev in range(8)]))
+    slot_portion = jnp.roll(
+        jnp.concatenate(ring[::-1], axis=1), (lax.axis_index("req") + 1) * ring[0].shape[1], axis=1
+    )
     offset = jnp.int32(0)
     amount = slot_portion.shape[1]
     key_index, key_request, key_position, key_adapter = token_info(

time: 495 us -> 598 us (1.21)
  waiting for transfers between devices: 316 us -> 369 us
  local copies, waits for them, and re-layouts: 32.5 us -> 73.5 us
  matrix products: 95.9 us -> 102 us
    ppermute x0 -> x7, waiting for transfers between devices: none -> 71.6 us  [per_device(): lax.ppermute(ring[-1], 'req', [(dev, (dev + 1) % 8) for dev in range(8)])]
    unnamed x23 -> x45, local copies, waits for them, and re-layouts: 2.09 us -> 26.7 us
    all_gather x1 -> x0, waiting for transfers between devices: 14 us -> none  [per_device(): slot_portion = lax.all_gather(paired, 'req', axis=1, tiled=True)]
    another operation x2, local copies, waits for them, and re-layouts: 12.1 us -> 21.5 us
  transfers between devices with their start and end apart: 5 -> 11, of which waited for: 5 -> 11; matrix products, arithmetic and copies ran while one was open for 10% -> 9% of each run, Pallas kernels for 0% -> 0%
where the time goes in v1:
time: 598 us; the launch traced here: 597 us
  waiting for transfers between devices  369 us (62%)
  matrix products  102 us (17%)
  local copies, waits for them, and re-layouts  73.5 us (12%)
  other arithmetic  36.8 us (6%)
  between operations  14.7 us (2%)
    reduce_scatter x1, waiting for transfers between devices, per_device(): lax.psum_scatter((rank_product(attention_output, output_rows) + (rank_pro...  84.4 us
    psum x1, waiting for transfers between devices, per_device(): rank_input = lax.psum(rank_part.astype(jnp.bfloat16), 'mlp')  80.1 us
    ppermute x7, waiting for transfers between devices, per_device(): lax.ppermute(ring[-1], 'req', [(dev, (dev + 1) % 8) for dev in range(8)])  71.6 us
    dot_general x10, matrix products, rank_product(): return jnp.dot(left_side, right_side, preferred_element_type=jnp.float32)  70.7 us
    psum x1, waiting for transfers between devices, per_device(): rank_output = lax.psum(rank_part_out.astype(jnp.bfloat16), 'mlp')  69.8 us
    all_gather x1, waiting for transfers between devices, per_device(): slot_portion = lax.all_gather(normed_rows, 'mlp', axis=0, tiled=True)  63.4 us
    unnamed x45, local copies, waits for them, and re-layouts  26.7 us
    another operation x2, local copies, waits for them, and re-layouts  21.5 us
  transfers between devices with their start and end apart: 11, of which 11 were waited for; matrix products, arithmetic and copies ran while one was open for 9% of the time, Pallas kernels for 0%

profile of v1, /device:TPU:0, one launch (start us, length us, event | category | flops | bytes accessed | tf_op | source)
XLA Modules:
  0.0 596.7 jit_solution(13528822115146618277)
XLA Ops:
  6.5 1.4 convert_reduce_fusion.1
  7.9 1.3 fusion.37
  9.3 2.1 fusion.40
  13.8 6.2 %gather_fusion = s32[1024]{0:T(1024)S(1)} fusion(s32[257]{0:T(512)} %param.36, s32[1024]{0:T(1024)S(1)} %maximum_clamp_fusion), kind=kCustom, calls=%fused_computation | custom fusion | bytes 12288 | tf_op jit(solution)/shard_map/jit(_take)/gather | solution.py:34
  21.5 63.4 %all-gather.2.cloned.1.call-done = bf16[1024,4096]{1,0:T(8,128)(2,1)} async-done(((bf16[64,4096]{1,0:T(8,128)(2,1)}), bf16[1024,4096]{1,0:T(8,128)(2,1)}) %all-gather.2.cloned.1.call-update) | async-done | bytes 8388624 | tf_op jit(solution)/shard_map/all_gather | solution.py:102
  84.9 6.5 %fusion.69 = f32[1024,128]{0,1:T(8,128)S(1)} fusion(bf16[1024,4096]{1,0:T(8,128)(2,1)} %all-gather.2.cloned.1.call-done, bf16[4096,128]{1,0:T(8,128)(2,1)} %param.29), kind=kOutput, calls=%fused_computation.131 | convolution fusion | flops 1073741824 | bytes 9961472 | tf_op jit(solution)/shard_map/dot_general | solution.py:16
  92.7 80.1 %all-reduce.4.cloned.1.call-done = bf16[1024,32]{0,1:T(8,128)(2,1)} async-done(((bf16[1024,32]{0,1:T(8,128)(2,1)}), bf16[1024,32]{0,1:T(8,128)(2,1)}) %all-reduce.4.cloned.1.call-update) | async-done | bytes 65552 | tf_op jit(solution)/shard_map/psum | solution.py:117
  173.6 1.7 broadcast_select_fusion
  175.3 3.3 fusion.31
  178.6 11.2 %fusion.68 = (bf16[1024,1,768]{0,2,1:T(8,128)(2,1)S(1)}, f32[1024,1,768]{0,2,1:T(8,128)S(1)}) fusion(f32[1024,768]{0,1:T(8,128)S(1)} %fusion.31, bf16[1024,4096]{1,0:T(8,128)(2,1)} %all-gather.2.cloned.1.call-done, bf16[4096,1,768]{2,0,1:T(8,128)(2,1)} %param.23), kind=kOutput, calls=%fused_computation.130 | convolution fusion | flops 6444023808 | bytes 22544384 | tf_op jit(solution)/shard_map/dot_general | solution.py:16
  190.8 2.0 reshape.592
  192.7 1.7 fusion.65
  194.4 2.0 reshape.591
  197.3 2.2 fusion.59
  201.4 15.4 %collective-permute-done = bf16[2,1024,256]{1,2,0:T(8,128)(2,1)S(1)} collective-permute-done((bf16[2,1024,256]{1,2,0:T(8,128)(2,1)S(1)}, bf16[2,1024,256]{1,2,0:T(8,128)(2,1)S(1)}, u32[]{:S(2)}, u32[]{:S(2)}) %collective-permute-start) | collective-permute-done | bytes 1048608 | tf_op jit(solution)/shard_map/ppermute | solution.py:153
  217.8 15.4 %collective-permute-done.1 = bf16[2,1024,256]{1,2,0:T(8,128)(2,1)S(1)} collective-permute-done((bf16[2,1024,256]{1,2,0:T(8,128)(2,1)S(1)}, bf16[2,1024,256]{1,2,0:T(8,128)(2,1)S(1)}, u32[]{:S(2)}, u32[]{:S(2)}) %collective-permute-start.1) | collective-permute-done | bytes 1048608 | tf_op jit(solution)/shard_map/ppermute | solution.py:153
  234.2 15.5 %collective-permute-done.2 = bf16[2,1024,256]{1,2,0:T(8,128)(2,1)} collective-permute-done((bf16[2,1024,256]{1,2,0:T(8,128)(2,1)S(1)}, bf16[2,1024,256]{1,2,0:T(8,128)(2,1)}, u32[]{:S(2)}, u32[]{:S(2)}) %collective-permute-start.2) | collective-permute-done | bytes 1048608 | tf_op jit(solution)/shard_map/ppermute | solution.py:153
  250.3 1.3 convert_reduce_fusion
  254.2 2.0 copy.51
  256.2 9.3 %collective-permute-done.3 = bf16[2,1024,256]{1,2,0:T(8,128)(2,1)} collective-permute-done((bf16[2,1024,256]{1,2,0:T(8,128)(2,1)}, bf16[2,1024,256]{1,2,0:T(8,128)(2,1)}, u32[]{:S(2)}, u32[]{:S(2)}) %collective-permute-start.3) | collective-permute-done | bytes 1048608 | tf_op jit(solution)/shard_map/ppermute | solution.py:153
  265.5 10.4 %fusion.70 = f32[1024,512]{1,0:T(8,128)} fusion(bf16[1024,4096]{1,0:T(8,128)(2,1)} %all-gather.2.cloned.1.call-done, bf16[4096,512]{1,0:T(8,128)(2,1)} %param.25), kind=kOutput, calls=%fused_computation.132 | convolution fusion | flops 4294967296 | bytes 14680064 | tf_op jit(solution)/shard_map/dot_general | solution.py:16
  276.6 1.6 concatenate.45
  278.2 1.8 pad_maximum_fusion.1
  280.1 1.1 collective-permute-done.4
  281.2 4.4 fusion.26
  285.6 1.3 fusion.72
  287.0 2.4 fusion.18
  289.4 7.5 %collective-permute-done.5 = bf16[2,1024,256]{1,2,0:T(8,128)(2,1)S(1)} collective-permute-done((bf16[2,1024,256]{1,2,0:T(8,128)(2,1)}, bf16[2,1024,256]{1,2,0:T(8,128)(2,1)S(1)}, u32[]{:S(2)}, u32[]{:S(2)}) %collective-permute-start.5) | collective-permute-done | bytes 1048608 | tf_op jit(solution)/shard_map/ppermute | solution.py:153
  296.9 8.1 %fusion.71 = f32[1024,4096]{1,0:T(8,128)} fusion(bf16[1024,512]{1,0:T(8,128)(2,1)S(1)} %fusion.26, bf16[512,4096]{1,0:T(8,128)(2,1)S(1)} %copy-done.14), kind=kOutput, calls=%fused_computation.133 | convolution fusion | flops 4294967296 | bytes 22020096 | tf_op jit(solution)/shard_map/dot_general | solution.py:16
  304.9 7.4 %collective-permute-done.6 = bf16[2,1024,256]{1,2,0:T(8,128)(2,1)S(1)} collective-permute-done((bf16[2,1024,256]{1,2,0:T(8,128)(2,1)S(1)}, bf16[2,1024,256]{1,2,0:T(8,128)(2,1)S(1)}, u32[]{:S(2)}, u32[]{:S(2)}) %collective-permute-start.6) | collective-permute-done | bytes 1048608 | tf_op jit(solution)/shard_map/ppermute | solution.py:153
  314.3 2.3 constant_dynamic-update-slice_fusion.13
  316.7 2.3 constant_dynamic-update-slice_fusion.12
  319.0 2.3 constant_dynamic-update-slice_fusion.11
  326.5 2.3 constant_dynamic-update-slice_fusion.5
  328.8 2.3 constant_dynamic-update-slice_fusion.4
  331.0 2.3 constant_dynamic-update-slice_fusion.3
  336.5 70.3 %conditional.1 = (f32[1024,1]{0,1:T(1,128)S(1)}, f32[1024,1,256]{0,2,1:T(8,128)S(1)}) conditional(s32[]{:T(128)} %convert_element_type.86, () %tuple.24, (s32[8192]{0:T(1024)S(1)}, s32[1024]{0:T(1024)S(1)}, s32[8192]{0:T(1024)S(1)}, s32[]{:T(128)}, s32[1024]{0:T(1024)S(1)}, /*index=5*/s32[]{:T(128)}, s32[]{:T(128)}, ...), branch_computations={%region_9.10_spmd, %region_10.13_spmd.clone} | conditional | flops 8774483968 | bytes 280748288 | solution.py:187
  336.6 21.4 %copy.49 = bf16[2,16384,256]{2,1,0:T(8,128)(2,1)} copy(bf16[2,16384,256]{1,2,0:T(8,128)(2,1)} %get-tuple-element.216) | data formatting | bytes 33554432 | tf_op jit(solution)/shard_map
  358.0 14.7 %fusion = (f32[1024]{0:T(1024)S(1)}, f32[8192,1024]{1,0:T(8,128)}) fusion(s32[1024]{0:T(1024)S(1)} %broadcast_add_fusion, s32[1024]{0:T(1024)S(1)} %get-tuple-element.144, s32[8192]{0:T(1024)S(1)} %get-tuple-element.145, s32[8192]{0:T(1024)S(1)} %get-tuple-element.143, bf16[1024,1,256]{0,2,1:T(8,128)(2,1)S(1)} %copy-done.8, ...), kind=kOutput, calls=%fused_computation.4 | convolution fusion | flops 4345297920 | bytes 38350852 | tf_op jit(solution)/shard_map/cond/branch_1_fun/qhd,khd->qhk/dot_general | solution.py:169
  372.7 16.6 %fusion.7 = f32[1024,1,256]{0,2,1:T(8,128)S(1)} fusion(f32[8192,1024]{1,0:T(8,128)} %get-tuple-element.225, f32[1024]{0:T(1024)S(1)} %broadcast_maximum_fusion, s32[1024]{0:T(1024)S(1)} %broadcast_add_fusion, s32[1024]{0:T(1024)S(1)} %get-tuple-element.144, s32[8192]{0:T(1024)S(1)} %get-tuple-element.145, s32[8192]{0:T(1024)S(1)} %get-tuple-element.143, ...), kind=kOutput, calls=%fused_computation.12 | convolution fusion | flops 4362076160 | bytes 38875144 | tf_op jit(solution)/shard_map/cond/branch_1_fun/qhk,khd->qhd/dot_general | solution.py:179
  389.3 4.8 copy-done.1
  394.1 12.7 %fusion.2 = f32[1024]{0:T(1024)S(1)} fusion(f32[8192,1024]{1,0:T(8,128)S(1)} %copy-done.1, f32[1024]{0:T(1024)S(1)} %broadcast_maximum_fusion, s32[1024]{0:T(1024)S(1)} %broadcast_add_fusion, s32[1024]{0:T(1024)S(1)} %get-tuple-element.144, s32[8192]{0:T(1024)S(1)} %get-tuple-element.145, s32[8192]{0:T(1024)S(1)} %get-tuple-element.143), kind=kLoop, calls=%fused_computation.6 | loop fusion | flops 67107840 | bytes 33636352 | tf_op jit(solution)/shard_map/cond/branch_1_fun/reduce_sum | solution.py:178
  406.8 1.8 multiply_reduce_fusion
  409.3 8.1 %fusion.27 = f32[1024,4096]{1,0:T(8,128)} fusion(bf16[1,256,4096]{2,1,0:T(8,128)(2,1)S(1)} %copy-done, f32[1024,1,256]{0,2,1:T(8,128)S(1)} %get-tuple-element.135, f32[1024]{0:T(1024)S(1)} %bitcast.115), kind=kOutput, calls=%fused_computation.39 | convolution fusion | flops 2148007936 | bytes 19927040 | tf_op jit(solution)/shard_map/dot_general | solution.py:16
  417.5 69.8 %all-reduce.6.cloned.1.call-done = bf16[1024,32]{0,1:T(8,128)(2,1)} async-done(((bf16[1024,32]{0,1:T(8,128)(2,1)}), bf16[1024,32]{0,1:T(8,128)(2,1)}) %all-reduce.6.cloned.1.call-update) | async-done | bytes 65552 | tf_op jit(solution)/shard_map/psum | solution.py:206
  488.1 15.6 %add_convert_fusion = bf16[1024,4096]{1,0:T(8,128)(2,1)} fusion(f32[1024,4096]{1,0:T(8,128)} %fusion.27, f32[1024,4096]{1,0:T(8,128)} %fusion.71, bf16[1024,128]{0,1:T(8,128)(2,1)S(1)} %bitcast.111, bf16[128,4096]{1,0:T(8,128)(2,1)} %param.34), kind=kOutput, calls=%fused_computation.21 | convolution fusion | flops 1086324736 | bytes 43253760 | tf_op jit(solution)/shard_map/dot_general | solution.py:16
  503.8 84.4 %reduce-scatter.2.cloned.1.call-done = bf16[64,4096]{1,0:T(8,128)(2,1)} async-done(((bf16[1024,4096]{1,0:T(8,128)(2,1)}), bf16[64,4096]{1,0:T(8,128)(2,1)}) %reduce-scatter.2.cloned.1.call-update) | async-done | bytes 524304 | tf_op jit(solution)/shard_map/reduce_scatter | solution.py:208
  588.2 2.0 fusion.42
  (96 shorter events, 26.3 us)
Async XLA Ops:
  6.5 402.8 %copy-start = (bf16[1,256,4096]{2,1,0:T(8,128)(2,1)S(1)}, bf16[1,256,4096]{2,1,0:T(8,128)(2,1)}, u32[]{:S(2)}) copy-start(bf16[1,256,4096]{2,1,0:T(8,128)(2,1)} %param.24) | copy-start | bytes 6291460
  6.5 78.4 %all-gather.2.cloned.1.call-start = ((), (), s32[]{:S(2)}) async-start(), calls=%async_computation.1 | async-start | bytes 8912896 | tf_op jit(solution)/shard_map/all_gather | solution.py:102
  11.4 161.4 %all-reduce.4.cloned.1.call-start = ((), (), s32[]{:S(2)}) async-start(), calls=%async_computation.2 | async-start | bytes 131072 | tf_op jit(solution)/shard_map/psum | solution.py:117
  92.1 395.1 %all-reduce.6.cloned.1.call-start = ((), (), s32[]{:S(2)}) async-start(), calls=%async_computation.3 | async-start | bytes 131072 | tf_op jit(solution)/shard_map/psum | solution.py:206
  201.3 15.4 %collective-permute-start = (bf16[2,1024,256]{1,2,0:T(8,128)(2,1)S(1)}, bf16[2,1024,256]{1,2,0:T(8,128)(2,1)S(1)}, u32[]{:S(2)}, u32[]{:S(2)}) collective-permute-start(bf16[2,1024,256]{1,2,0:T(8,128)(2,1)S(1)} %pad_maximum_fusion), channel_id=1, source_target_pairs={{0,16},{16,32},{32,48},{48,64},{64,80},{80,96},{96,112},{112,0},{1... | collective-permute-start | bytes 3145736 | tf_op jit(solution)/shard_map/ppermute | solution.py:153
  216.8 1.0 copy-start.3
  217.8 15.4 %collective-permute-start.1 = (bf16[2,1024,256]{1,2,0:T(8,128)(2,1)S(1)}, bf16[2,1024,256]{1,2,0:T(8,128)(2,1)S(1)}, u32[]{:S(2)}, u32[]{:S(2)}) collective-permute-start(bf16[2,1024,256]{1,2,0:T(8,128)(2,1)S(1)} %collective-permute-done), channel_id=1, source_target_pairs={{0,16},{16,32},{32,48},{48,64},{64,80},{80,96},{96,112},{112,0},{1... | collective-permute-start | bytes 3145736 | tf_op jit(solution)/shard_map/ppermute | solution.py:153
  233.2 1.0 copy-start.5
  234.2 15.5 %collective-permute-start.2 = (bf16[2,1024,256]{1,2,0:T(8,128)(2,1)S(1)}, bf16[2,1024,256]{1,2,0:T(8,128)(2,1)}, u32[]{:S(2)}, u32[]{:S(2)}) collective-permute-start(bf16[2,1024,256]{1,2,0:T(8,128)(2,1)S(1)} %collective-permute-done.1), channel_id=1, source_target_pairs={{0,16},{16,32},{32,48},{48,64},{64,80},{80,96},{96,112},{112,0},{1... | collective-permute-start | bytes 3145736 | tf_op jit(solution)/shard_map/ppermute | solution.py:153
  249.7 15.8 %collective-permute-start.3 = (bf16[2,1024,256]{1,2,0:T(8,128)(2,1)}, bf16[2,1024,256]{1,2,0:T(8,128)(2,1)}, u32[]{:S(2)}, u32[]{:S(2)}) collective-permute-start(bf16[2,1024,256]{1,2,0:T(8,128)(2,1)} %collective-permute-done.2), channel_id=1, source_target_pairs={{0,16},{16,32},{32,48},{48,64},{64,80},{80,96},{96,112},{112,0},{1... | collective-permute-start | bytes 3145736 | tf_op jit(solution)/shard_map/ppermute | solution.py:153
  251.6 0.6 copy-start.11
  256.2 19.6 %copy-start.9 = (bf16[1024,1,32,1]{0,2,3,1:T(8,128)(2,1)S(1)}, bf16[1024,1,32,1]{0,2,3,1:T(8,128)(2,1)}, u32[]{:S(2)}) copy-start(bf16[1024,1,32,1]{0,2,3,1:T(8,128)(2,1)} %get-tuple-element.230) | copy-start | bytes 196612
  256.2 19.6 %copy-start.10 = (bf16[1024,1,32,1]{0,2,3,1:T(8,128)(2,1)S(1)}, bf16[1024,1,32,1]{0,2,3,1:T(8,128)(2,1)}, u32[]{:S(2)}) copy-start(bf16[1024,1,32,1]{0,2,3,1:T(8,128)(2,1)} %get-tuple-element.231) | copy-start | bytes 196612
  256.2 25.0 %copy-start.16 = (f32[512]{0:T(512)S(1)}, f32[512]{0:T(512)}, u32[]{:S(2)}) copy-start(f32[512]{0:T(512)} %param.26) | copy-start | bytes 6148
  265.5 15.8 %collective-permute-start.4 = (bf16[2,1024,256]{1,2,0:T(8,128)(2,1)}, bf16[2,1024,256]{1,2,0:T(8,128)(2,1)}, u32[]{:S(2)}, u32[]{:S(2)}) collective-permute-start(bf16[2,1024,256]{1,2,0:T(8,128)(2,1)} %collective-permute-done.3), channel_id=1, source_target_pairs={{0,16},{16,32},{32,48},{48,64},{64,80},{80,96},{96,112},{112,0},{1... | collective-permute-start | bytes 3145736 | tf_op jit(solution)/shard_map/ppermute | solution.py:153
  278.2 7.4 %copy-start.15 = (bf16[512,1024]{1,0:T(8,128)(2,1)S(1)}, bf16[512,1024]{1,0:T(8,128)(2,1)}, u32[]{:S(2)}) copy-start(bf16[512,1024]{1,0:T(8,128)(2,1)} %param.33) | copy-start | bytes 3145732
  281.2 15.6 %collective-permute-start.5 = (bf16[2,1024,256]{1,2,0:T(8,128)(2,1)}, bf16[2,1024,256]{1,2,0:T(8,128)(2,1)S(1)}, u32[]{:S(2)}, u32[]{:S(2)}) collective-permute-start(bf16[2,1024,256]{1,2,0:T(8,128)(2,1)} %collective-permute-done.4), channel_id=1, source_target_pairs={{0,16},{16,32},{32,48},{48,64},{64,80},{80,96},{96,112},{112,0},{1... | collective-permute-start | bytes 3145736 | tf_op jit(solution)/shard_map/ppermute | solution.py:153
  281.2 5.8 copy-start.7
  285.6 11.2 %copy-start.14 = (bf16[512,4096]{1,0:T(8,128)(2,1)S(1)}, bf16[512,4096]{1,0:T(8,128)(2,1)}, u32[]{:S(2)}) copy-start(bf16[512,4096]{1,0:T(8,128)(2,1)} %param.27) | copy-start | bytes 12582916
  296.9 15.4 %collective-permute-start.6 = (bf16[2,1024,256]{1,2,0:T(8,128)(2,1)S(1)}, bf16[2,1024,256]{1,2,0:T(8,128)(2,1)S(1)}, u32[]{:S(2)}, u32[]{:S(2)}) collective-permute-start(bf16[2,1024,256]{1,2,0:T(8,128)(2,1)S(1)} %collective-permute-done.5), channel_id=1, source_target_pairs={{0,16},{16,32},{32,48},{48,64},{64,80},{80,96},{96,112},{112,0},{1... | collective-permute-start | bytes 3145736 | tf_op jit(solution)/shard_map/ppermute | solution.py:153
  304.9 16.3 %copy-start.6 = (bf16[2,1024,256]{1,2,0:T(8,128)(2,1)S(1)}, bf16[2,1024,256]{1,2,0:T(8,128)(2,1)}, u32[]{:S(2)}) copy-start(bf16[2,1024,256]{1,2,0:T(8,128)(2,1)} %copy-done.5) | copy-start | bytes 3145732
  304.9 17.3 %copy-start.4 = (bf16[2,1024,256]{1,2,0:T(8,128)(2,1)S(1)}, bf16[2,1024,256]{1,2,0:T(8,128)(2,1)}, u32[]{:S(2)}) copy-start(bf16[2,1024,256]{1,2,0:T(8,128)(2,1)} %copy-done.3) | copy-start | bytes 3145732
  324.4 12.1 %copy-start.12 = (s32[8192]{0:T(1024)S(1)}, s32[8192]{0:T(1024)}, u32[]{:S(2)}) copy-start(s32[8192]{0:T(1024)} %copy-done.11) | copy-start | bytes 98308
  336.6 21.4 %copy-start.8 = (bf16[1024,1,256]{0,2,1:T(8,128)(2,1)S(1)}, bf16[1024,1,256]{0,2,1:T(8,128)(2,1)}, u32[]{:S(2)}) copy-start(bf16[1024,1,256]{0,2,1:T(8,128)(2,1)} %get-tuple-element.217) | copy-start | bytes 1572868 | tf_op jit(solution)/shard_map/cond
  372.7 21.4 %copy-start.1 = (f32[8192,1024]{1,0:T(8,128)S(1)}, f32[8192,1024]{1,0:T(8,128)}, u32[]{:S(2)}) copy-start(f32[8192,1024]{1,0:T(8,128)} %get-tuple-element.225) | copy-start | bytes 100663296 | tf_op jit(solution)/shard_map/cond
  409.3 178.9 %reduce-scatter.2.cloned.1.call-start = ((), (), s32[]{:S(2)}) async-start(), calls=%async_computation.4 | async-start | bytes 8912896 | tf_op jit(solution)/shard_map/reduce_scatter | solution.py:208
  503.8 84.5 %copy-start.2 = (bf16[64,4096]{1,0:T(8,128)(2,1)S(1)}, bf16[64,4096]{1,0:T(8,128)(2,1)}, u32[]{:S(2)}) copy-start(bf16[64,4096]{1,0:T(8,128)(2,1)} %param.20) | copy-start | bytes 1572868
  503.8 84.5 %copy-start.13 = (f32[4096]{0:T(1024)S(1)}, f32[4096]{0:T(1024)}, u32[]{:S(2)}) copy-start(f32[4096]{0:T(1024)} %param.28) | copy-start | bytes 49156
Sparse Core Ops, SparseCore 0:
  11.5 73.3 all-gather.1
  92.2 80.5 all-reduce.3
  409.4 77.8 all-reduce.5
  503.9 84.2 reduce-scatter.1
